TPU v7x, 512 devices: a whole 4x8x8 slice. The times are simulated.
512 devices in a mesh: rows: 64 (over x, y, core), vec: 8 (over z).
Axes of the slice: x: 4, y: 8, z: 8, core: 2. Of those that a mesh axis runs over, the one named last changes fastest.
Arguments:
- vectors: float32 [64, 131072], P('vec', 'rows'), may hold values from -6 to 6
- damage: float32 [131072], P('rows')
- diag_blocks: bfloat16 [1024, 128, 128], P('rows')
- upper_blocks: bfloat16 [8192, 128, 128], P('rows'), may hold values from -0.5 to 0.5
- block_rows: int32 [8192], P('rows'), may hold values from 0 to 1023, as said below
- block_cols: int32 [8192], P('rows'), may hold values from 1 to 1023, as said below
- live_slots: int32 [64], P('rows'), may hold values from 64 to 128, as said below
Outputs:
- product: float32 [64, 131072], P('vec', 'rows')
- projected: float32 [64, 64], P('vec')
Inputs may be any that keep to these rules, and one draw needn't show every extreme that they name: `block_rows`: the slots of device d name block rows d * 16 to (d + 1) * 16 - 1; a slot whose column lies on another device names one of the last 6 of these. block_cols[s] is greater than block_rows[s], and block_cols[s] // 16 lies between d and d + 3 for a slot of device d; some slots reach d + 3. A column on device e other than d is one of the first 6 block rows of e. A pair may appear in several slots; their blocks add. `live_slots`: some device has all its slots stored.
All inputs are finite; a program needn't handle non-finite values.
Results may differ from a plain program's by a relative error of at most 0.0029.
Values may be sent and summed in bfloat16 or wider, within the bound.
No kernel may reach another device: no remote copies, remote signals or barrier semaphores. Data moves between devices by JAX's collectives and lax.ppermute only.
A program may use at most 64 MiB of HBM per device.

v0:
```python
import jax
import jax.numpy as jnp
from jax import lax
from jax.sharding import PartitionSpec as P

REACH = 4
RIM = 6
resid_eta = 0.001


def passed_along(array, axis, by):
    devices = lax.axis_size(axis)
    pairs = [(i, i + by) for i in range(devices) if 0 <= i + by < devices]
    return lax.ppermute(array, axis, pairs)


def on_device(vectors, damage, diag_blocks, upper_blocks, block_rows, block_cols, live_slots):
    vec_here, width = vectors.shape
    rb_here = diag_blocks.shape[0]
    block_size = diag_blocks.shape[1]
    slot_count = upper_blocks.shape[0]
    mine = lax.axis_index("rows")
    soft = jnp.sqrt((1.0 - damage) ** 2 + resid_eta)
    scaled = (vectors * soft[None, :]).astype(jnp.bfloat16).reshape(vec_here, rb_here, block_size)
    stored = (jnp.arange(slot_count) < live_slots[0]).astype(jnp.float32)
    local_rows = block_rows - mine * rb_here
    row_pick = (local_rows[:, None] == jnp.arange(rb_here)[None, :]).astype(jnp.float32) * stored[
        :, None
    ]
    own_rows = jnp.einsum(
        "vrb,sr->vsb", scaled, row_pick.astype(jnp.bfloat16), preferred_element_type=jnp.float32
    ).astype(jnp.bfloat16)
    accum = jnp.einsum("vrj,rij->vri", scaled, diag_blocks, preferred_element_type=jnp.float32)
    backward = jnp.einsum(
        "vsi,sij->vsj", own_rows, upper_blocks, preferred_element_type=jnp.float32
    )
    pieces = [scaled]
    for step in range(1, REACH):
        pieces.append(passed_along(scaled[:, :RIM], "rows", -step))
    window = jnp.concatenate(pieces, axis=1)
    relative = block_cols - mine * rb_here
    dev_step = relative // rb_here
    within = relative - dev_step * rb_here
    col_index = jnp.where(dev_step == 0, within, rb_here + (dev_step - 1) * RIM + within)
    span = window.shape[1]
    col_pick = (col_index[:, None] == jnp.arange(span)[None, :]).astype(jnp.float32) * stored[
        :, None
    ]
    far_cols = jnp.einsum(
        "vcb,sc->vsb", window, col_pick.astype(jnp.bfloat16), preferred_element_type=jnp.float32
    ).astype(jnp.bfloat16)
    forward = jnp.einsum("vsj,sij->vsi", far_cols, upper_blocks, preferred_element_type=jnp.float32)
    gathered = jnp.einsum("vsi,sr->vri", forward, row_pick, precision=lax.Precision.HIGHEST)
    spread = jnp.einsum("vsj,sc->vcj", backward, col_pick, precision=lax.Precision.HIGHEST)
    gathered, spread = (gathered, spread)
    accum = accum + gathered + spread[:, :rb_here]
    for step in range(1, REACH):
        low = rb_here + (step - 1) * RIM
        arrived = passed_along(spread[:, low : low + RIM], "rows", step)
        accum = accum.at[:, :RIM].add(arrived)
    product = soft[None, :] * accum.reshape(vec_here, width)
    partial_gram = jnp.dot(
        vectors,
        lax.all_gather(product.astype(jnp.bfloat16), "vec", axis=0, tiled=True)
        .astype(jnp.float32)
        .T,
        precision=lax.Precision.HIGHEST,
        preferred_element_type=jnp.float32,
    )
    total_dof = width * lax.axis_size("rows")
    projected = lax.psum(partial_gram, "rows") / total_dof
    return (product, projected)


def solution(mesh):
    return jax.shard_map(
        on_device,
        mesh=mesh,
        in_specs=(
            P("vec", "rows"),
            P("rows"),
            P("rows", None, None),
            P("rows", None, None),
            P("rows"),
            P("rows"),
            P("rows"),
        ),
        out_specs=(P("vec", "rows"), P("vec", None)),
        check_vma=False,
    )
```

profile of v0, /device:TPU:1, one launch (start us, length us, event | category | flops | bytes accessed | tf_op | source)
XLA Modules:
  0.0 186.2 jit_solution(1229719728883084545)
XLA Ops:
  0.6 0.0 copy-start
  0.6 0.8 add_sqrt_fusion
  1.4 0.9 fusion.16
  2.3 1.3 collective-permute-start.2
  3.6 1.3 collective-permute-start.1
  4.9 8.8 %collective-permute-start = (bf16[8,6,128]{2,0,1:T(8,128)(2,1)S(1)}, bf16[8,6,128]{2,0,1:T(8,128)(2,1)S(1)}, u32[]{:S(2)}, u32[]{:S(2)}) collective-permute-start(bf16[8,6,128]{2,0,1:T(8,128)(2,1)S(1)} %slice.91), channel_id=1, source_target_pairs={{8,0},{16,8},{24,16},{32,24},{40,32},{48,40},{56,48},{64,56},{72,6... | collective-permute-start | bytes 36872 | tf_op jit(solution)/shard_map/ppermute | solution.py:14
  14.3 0.0 copy-start.1
  14.3 0.8 broadcast_subtract_fusion
  15.2 0.8 compare_select_fusion
  16.0 0.3 fusion.17
  16.3 3.4 %fusion.12 = f32[128,8,128]{2,1,0:T(8,128)S(1)} fusion(bf16[128,128,128]{2,1,0:T(8,128)(2,1)} %param.16, bf16[128,8,128]{2,0,1:T(8,128)(2,1)S(1)} %fusion.17), kind=kOutput, calls=%fused_computation.15 | convolution fusion | flops 33554432 | bytes 4980736 | tf_op jit(solution)/shard_map/vsi,sij->vsj/dot_general | solution.py:34
  19.7 0.5 fusion.2
  20.1 0.0 copy-start.2
  20.2 6.0 %collective-permute-start.5 = (f32[8,6,128]{2,0,1:T(8,128)S(1)}, f32[8,6,128]{2,0,1:T(8,128)S(1)}, u32[]{:S(2)}, u32[]{:S(2)}) collective-permute-start(f32[8,6,128]{2,0,1:T(8,128)S(1)} %get-tuple-element.40), channel_id=1, source_target_pairs={{0,24},{8,32},{16,40},{24,48},{32,56},{40,64},{48,72},{56,80},{64,... | collective-permute-start | bytes 73736 | tf_op jit(solution)/shard_map/ppermute | solution.py:14
  26.2 3.4 %collective-permute-start.4 = (f32[8,6,128]{2,0,1:T(8,128)S(1)}, f32[8,6,128]{2,0,1:T(8,128)S(1)}, u32[]{:S(2)}, u32[]{:S(2)}) collective-permute-start(f32[8,6,128]{2,0,1:T(8,128)S(1)} %get-tuple-element.41), channel_id=1, source_target_pairs={{0,16},{8,24},{16,32},{24,40},{32,48},{40,56},{48,64},{56,72},{64,... | collective-permute-start | bytes 73736 | tf_op jit(solution)/shard_map/ppermute | solution.py:14
  29.5 0.0 collective-permute-done.2
  29.5 1.9 %collective-permute-start.3 = (f32[8,6,128]{2,0,1:T(8,128)S(1)}, f32[8,6,128]{2,0,1:T(8,128)S(1)}, u32[]{:S(2)}, u32[]{:S(2)}) collective-permute-start(f32[8,6,128]{2,0,1:T(8,128)S(1)} %get-tuple-element.42), channel_id=1, source_target_pairs={{0,8},{8,16},{16,24},{24,32},{32,40},{40,48},{48,56},{56,64},{64,7... | collective-permute-start | bytes 73736 | tf_op jit(solution)/shard_map/ppermute | solution.py:14
  31.5 0.0 collective-permute-done.1
  31.5 0.0 collective-permute-done
  31.5 0.3 fusion.14
  31.8 0.0 copy-done.1
  31.8 2.3 %fusion.9 = f32[128,8,128]{2,1,0:T(8,128)S(1)} fusion(bf16[128,128,128]{2,1,0:T(8,128)(2,1)S(1)} %copy-done.1, bf16[128,8,128]{2,0,1:T(8,128)(2,1)S(1)} %fusion.14), kind=kOutput, calls=%fused_computation.13 | convolution fusion | flops 33554432 | bytes 4980736 | tf_op jit(solution)/shard_map/vsj,sij->vsi/dot_general | solution.py:52
  34.0 0.4 fusion.4
  34.5 0.4 fusion.1
  34.9 0.0 collective-permute-done.3
  34.9 0.0 collective-permute-done.4
  34.9 0.0 collective-permute-done.5
  34.9 0.6 fusion.39
  35.6 20.4 %all_gather.3 = bf16[64,2048]{1,0:T(8,128)(2,1)S(1)} all-gather(bf16[8,2048]{1,0:T(8,128)(2,1)S(1)} %get-tuple-element.38), channel_id=1, replica_groups=mesh['rows'=64,'vec'=8] {'vec'}, dimensions={0}, use_global_device_ids=true | all-gather | bytes 294912 | tf_op jit(solution)/shard_map/all_gather | solution.py:64
  56.0 0.3 convolution_bitcast_fusion
  56.3 129.3 %psum.7 = f32[8,64]{1,0:T(8,128)S(1)} all-reduce(f32[8,64]{1,0:T(8,128)S(1)} %convolution_bitcast_fusion), channel_id=1, replica_groups=mesh['rows'=64,'vec'=8] {'rows'}, use_global_device_ids=true, to_apply=%region_0.1 | all-reduce | flops 512 | bytes 4096 | tf_op jit(solution)/shard_map/psum | solution.py:71
  185.6 0.6 broadcast_multiply_fusion
  (11 shorter events, 0.1 us)
Async XLA Ops:
  0.6 33.8 %copy-start = (bf16[16,128,128]{2,1,0:T(8,128)(2,1)S(1)}, bf16[16,128,128]{2,1,0:T(8,128)(2,1)}, u32[]{:S(2)}) copy-start(bf16[16,128,128]{2,1,0:T(8,128)(2,1)} %param.15) | copy-start | bytes 1572868
  2.3 27.2 %collective-permute-start.2 = (bf16[8,6,128]{2,0,1:T(8,128)(2,1)S(1)}, bf16[8,6,128]{2,0,1:T(8,128)(2,1)S(1)}, u32[]{:S(2)}, u32[]{:S(2)}) collective-permute-start(bf16[8,6,128]{2,0,1:T(8,128)(2,1)S(1)} %slice.91), channel_id=1, source_target_pairs={{24,0},{32,8},{40,16},{48,24},{56,32},{64,40},{72,48},{80,56},{88,... | collective-permute-start | bytes 36872 | tf_op jit(solution)/shard_map/ppermute | solution.py:14
  3.6 27.9 %collective-permute-start.1 = (bf16[8,6,128]{2,0,1:T(8,128)(2,1)S(1)}, bf16[8,6,128]{2,0,1:T(8,128)(2,1)S(1)}, u32[]{:S(2)}, u32[]{:S(2)}) collective-permute-start(bf16[8,6,128]{2,0,1:T(8,128)(2,1)S(1)} %slice.91), channel_id=1, source_target_pairs={{16,0},{24,8},{32,16},{40,24},{48,32},{56,40},{64,48},{72,56},{80,... | collective-permute-start | bytes 36872 | tf_op jit(solution)/shard_map/ppermute | solution.py:14
  4.9 26.6 %collective-permute-start = (bf16[8,6,128]{2,0,1:T(8,128)(2,1)S(1)}, bf16[8,6,128]{2,0,1:T(8,128)(2,1)S(1)}, u32[]{:S(2)}, u32[]{:S(2)}) collective-permute-start(bf16[8,6,128]{2,0,1:T(8,128)(2,1)S(1)} %slice.91), channel_id=1, source_target_pairs={{8,0},{16,8},{24,16},{32,24},{40,32},{48,40},{56,48},{64,56},{72,6... | collective-permute-start | bytes 36872 | tf_op jit(solution)/shard_map/ppermute | solution.py:14
  14.3 17.4 %copy-start.1 = (bf16[128,128,128]{2,1,0:T(8,128)(2,1)S(1)}, bf16[128,128,128]{2,1,0:T(8,128)(2,1)}, u32[]{:S(2)}) copy-start(bf16[128,128,128]{2,1,0:T(8,128)(2,1)} %param.16) | copy-start | bytes 12582916
  20.1 35.9 %copy-start.2 = (f32[8,2048]{1,0:T(8,128)S(1)}, f32[8,2048]{1,0:T(8,128)}, u32[]{:S(2)}) copy-start(f32[8,2048]{1,0:T(8,128)} %param.13) | copy-start | bytes 196612
  20.2 14.7 %collective-permute-start.5 = (f32[8,6,128]{2,0,1:T(8,128)S(1)}, f32[8,6,128]{2,0,1:T(8,128)S(1)}, u32[]{:S(2)}, u32[]{:S(2)}) collective-permute-start(f32[8,6,128]{2,0,1:T(8,128)S(1)} %get-tuple-element.40), channel_id=1, source_target_pairs={{0,24},{8,32},{16,40},{24,48},{32,56},{40,64},{48,72},{56,80},{64,... | collective-permute-start | bytes 73736 | tf_op jit(solution)/shard_map/ppermute | solution.py:14
  26.2 8.7 %collective-permute-start.4 = (f32[8,6,128]{2,0,1:T(8,128)S(1)}, f32[8,6,128]{2,0,1:T(8,128)S(1)}, u32[]{:S(2)}, u32[]{:S(2)}) collective-permute-start(f32[8,6,128]{2,0,1:T(8,128)S(1)} %get-tuple-element.41), channel_id=1, source_target_pairs={{0,16},{8,24},{16,32},{24,40},{32,48},{40,56},{48,64},{56,72},{64,... | collective-permute-start | bytes 73736 | tf_op jit(solution)/shard_map/ppermute | solution.py:14
  29.5 5.3 %collective-permute-start.3 = (f32[8,6,128]{2,0,1:T(8,128)S(1)}, f32[8,6,128]{2,0,1:T(8,128)S(1)}, u32[]{:S(2)}, u32[]{:S(2)}) collective-permute-start(f32[8,6,128]{2,0,1:T(8,128)S(1)} %get-tuple-element.42), channel_id=1, source_target_pairs={{0,8},{8,16},{16,24},{24,32},{32,40},{40,48},{48,56},{56,64},{64,7... | collective-permute-start | bytes 73736 | tf_op jit(solution)/shard_map/ppermute | solution.py:14
where the time goes:
time: 187 us; the launch traced here: 186 us
  blocking collectives  150 us (80%)
  starting transfers between devices  22.6 us (12%)
  matrix products  7.72 us (4%)
  other arithmetic  4.55 us (2%)
    psum x1, blocking collectives, on_device(): projected = lax.psum(partial_gram, 'rows') / total_dof  129 us
    ppermute x6, starting transfers between devices, passed_along(): return lax.ppermute(array, axis, pairs)  22.6 us
    all_gather x1, blocking collectives, on_device(): lax.all_gather(product.astype(jnp.bfloat16), 'vec', axis=0, tiled=True)  20.4 us
  transfers between devices with their start and end apart: 6, of which 0 were waited for; matrix products, arithmetic and copies ran while one was open for 5% of the time, Pallas kernels for 0%

commit v1 on v0

--- a/solution.py
+++ b/solution.py
@@ -68,7 +68,7 @@
         preferred_element_type=jnp.float32,
     )
     total_dof = width * lax.axis_size("rows")
-    projected = lax.psum(partial_gram, "rows") / total_dof
+    projected = jnp.sum(lax.all_gather(partial_gram, "rows"), axis=0) / total_dof
     return (product, projected)
 
 

time: 187 us -> 105 us (0.56)
  blocking collectives: 150 us -> 68.3 us
    psum x1 -> x0, blocking collectives: 129 us -> none  [on_device(): projected = lax.psum(partial_gram, 'rows') / total_dof]
    all_gather x0 -> x1, blocking collectives: none -> 47.9 us  [on_device(): lax.all_gather(partial_gram, 'rows')]
  transfers between devices with their start and end apart: 6 -> 6, of which waited for: 0 -> 0; matrix products, arithmetic and copies ran while one was open for 5% -> 9% of each run, Pallas kernels for 0% -> 0%
where the time goes in v1:
time: 105 us
  blocking collectives  68.3 us (65%)
  starting transfers between devices  22.6 us (22%)
  matrix products  7.72 us (7%)
  other arithmetic  4.62 us (4%)
  between operations  1.52 us (1%)
    all_gather x1, blocking collectives, on_device(): lax.all_gather(partial_gram, 'rows')  47.9 us
    ppermute x6, starting transfers between devices, passed_along(): return lax.ppermute(array, axis, pairs)  22.6 us
    all_gather x1, blocking collectives, on_device(): lax.all_gather(product.astype(jnp.bfloat16), 'vec', axis=0, tiled=True)  20.4 us
    dot_general x1, matrix products, on_device(): jnp.einsum('vsi,sij->vsj', own_rows, upper_blocks, preferred_element_type...  3.38 us
    dot_general x1, matrix products, on_device(): jnp.einsum('vsj,sij->vsi', far_cols, upper_blocks, preferred_element_type...  2.25 us
  transfers between devices with their start and end apart: 6, of which 0 were waited for; matrix products, arithmetic and copies ran while one was open for 9% of the time, Pallas kernels for 0%

profile of v1, /device:TPU:1, one launch (start us, length us, event | category | flops | bytes accessed | tf_op | source)
XLA Modules:
  0.0 104.9 jit_solution(13496637133949277237)
XLA Ops:
  0.6 0.0 copy-start
  0.6 0.8 add_sqrt_fusion
  1.4 0.9 fusion.16
  2.3 1.3 %collective-permute-start.2 = (bf16[8,6,128]{2,0,1:T(8,128)(2,1)S(1)}, bf16[8,6,128]{2,0,1:T(8,128)(2,1)S(1)}, u32[]{:S(2)}, u32[]{:S(2)}) collective-permute-start(bf16[8,6,128]{2,0,1:T(8,128)(2,1)S(1)} %slice.91), channel_id=1, source_target_pairs={{24,0},{32,8},{40,16},{48,24},{56,32},{64,40},{72,48},{80,56},{88,... | collective-permute-start | bytes 36872 | tf_op jit(solution)/shard_map/ppermute | solution.py:14
  3.6 1.3 %collective-permute-start.1 = (bf16[8,6,128]{2,0,1:T(8,128)(2,1)S(1)}, bf16[8,6,128]{2,0,1:T(8,128)(2,1)S(1)}, u32[]{:S(2)}, u32[]{:S(2)}) collective-permute-start(bf16[8,6,128]{2,0,1:T(8,128)(2,1)S(1)} %slice.91), channel_id=1, source_target_pairs={{16,0},{24,8},{32,16},{40,24},{48,32},{56,40},{64,48},{72,56},{80,... | collective-permute-start | bytes 36872 | tf_op jit(solution)/shard_map/ppermute | solution.py:14
  4.9 8.8 %collective-permute-start = (bf16[8,6,128]{2,0,1:T(8,128)(2,1)S(1)}, bf16[8,6,128]{2,0,1:T(8,128)(2,1)S(1)}, u32[]{:S(2)}, u32[]{:S(2)}) collective-permute-start(bf16[8,6,128]{2,0,1:T(8,128)(2,1)S(1)} %slice.91), channel_id=1, source_target_pairs={{8,0},{16,8},{24,16},{32,24},{40,32},{48,40},{56,48},{64,56},{72,6... | collective-permute-start | bytes 36872 | tf_op jit(solution)/shard_map/ppermute | solution.py:14
  14.3 0.0 copy-start.1
  14.3 0.8 broadcast_subtract_fusion
  15.2 0.8 compare_select_fusion
  16.0 0.3 fusion.17
  16.3 3.4 %fusion.12 = f32[128,8,128]{2,1,0:T(8,128)S(1)} fusion(bf16[128,128,128]{2,1,0:T(8,128)(2,1)} %param.16, bf16[128,8,128]{2,0,1:T(8,128)(2,1)S(1)} %fusion.17), kind=kOutput, calls=%fused_computation.15 | convolution fusion | flops 33554432 | bytes 4980736 | tf_op jit(solution)/shard_map/vsi,sij->vsj/dot_general | solution.py:34
  19.7 0.5 fusion.2
  20.1 0.0 copy-start.2
  20.2 6.0 %collective-permute-start.5 = (f32[8,6,128]{2,0,1:T(8,128)S(1)}, f32[8,6,128]{2,0,1:T(8,128)S(1)}, u32[]{:S(2)}, u32[]{:S(2)}) collective-permute-start(f32[8,6,128]{2,0,1:T(8,128)S(1)} %get-tuple-element.40), channel_id=1, source_target_pairs={{0,24},{8,32},{16,40},{24,48},{32,56},{40,64},{48,72},{56,80},{64,... | collective-permute-start | bytes 73736 | tf_op jit(solution)/shard_map/ppermute | solution.py:14
  26.2 3.4 %collective-permute-start.4 = (f32[8,6,128]{2,0,1:T(8,128)S(1)}, f32[8,6,128]{2,0,1:T(8,128)S(1)}, u32[]{:S(2)}, u32[]{:S(2)}) collective-permute-start(f32[8,6,128]{2,0,1:T(8,128)S(1)} %get-tuple-element.41), channel_id=1, source_target_pairs={{0,16},{8,24},{16,32},{24,40},{32,48},{40,56},{48,64},{56,72},{64,... | collective-permute-start | bytes 73736 | tf_op jit(solution)/shard_map/ppermute | solution.py:14
  29.5 0.0 collective-permute-done.2
  29.5 1.9 %collective-permute-start.3 = (f32[8,6,128]{2,0,1:T(8,128)S(1)}, f32[8,6,128]{2,0,1:T(8,128)S(1)}, u32[]{:S(2)}, u32[]{:S(2)}) collective-permute-start(f32[8,6,128]{2,0,1:T(8,128)S(1)} %get-tuple-element.42), channel_id=1, source_target_pairs={{0,8},{8,16},{16,24},{24,32},{32,40},{40,48},{48,56},{56,64},{64,7... | collective-permute-start | bytes 73736 | tf_op jit(solution)/shard_map/ppermute | solution.py:14
  31.5 0.0 collective-permute-done.1
  31.5 0.0 collective-permute-done
  31.5 0.3 fusion.14
  31.8 2.3 %fusion.9 = f32[128,8,128]{2,1,0:T(8,128)S(1)} fusion(bf16[128,128,128]{2,1,0:T(8,128)(2,1)S(1)} %copy-done.1, bf16[128,8,128]{2,0,1:T(8,128)(2,1)S(1)} %fusion.14), kind=kOutput, calls=%fused_computation.13 | convolution fusion | flops 33554432 | bytes 4980736 | tf_op jit(solution)/shard_map/vsj,sij->vsi/dot_general | solution.py:52
  34.0 0.4 fusion.4
  34.5 0.4 fusion.1
  34.9 0.0 collective-permute-done.3
  34.9 0.0 collective-permute-done.4
  34.9 0.0 collective-permute-done.5
  34.9 0.6 fusion.39
  35.6 20.4 %all_gather.9 = bf16[64,2048]{1,0:T(8,128)(2,1)S(1)} all-gather(bf16[8,2048]{1,0:T(8,128)(2,1)S(1)} %get-tuple-element.38), channel_id=1, replica_groups=mesh['rows'=64,'vec'=8] {'vec'}, dimensions={0}, use_global_device_ids=true | all-gather | bytes 294912 | tf_op jit(solution)/shard_map/all_gather | solution.py:64
  56.0 0.3 convolution_bitcast_fusion
  56.3 47.9 %all-gather = f32[512,64]{1,0:T(8,128)S(1)} all-gather(f32[8,64]{1,0:T(8,128)S(1)} %convolution_bitcast_fusion), channel_id=2, replica_groups=mesh['rows'=64,'vec'=8] {'rows'}, dimensions={0}, use_global_device_ids=true | all-gather | bytes 133120 | tf_op jit(solution)/shard_map/all_gather | solution.py:71
  104.2 0.1 bitcast_reduce_fusion
  104.3 0.6 broadcast_multiply_fusion
  (12 shorter events, 0.1 us)
Async XLA Ops:
  0.6 33.8 %copy-start = (bf16[16,128,128]{2,1,0:T(8,128)(2,1)S(1)}, bf16[16,128,128]{2,1,0:T(8,128)(2,1)}, u32[]{:S(2)}) copy-start(bf16[16,128,128]{2,1,0:T(8,128)(2,1)} %param.15) | copy-start | bytes 1572868
  2.3 27.2 %collective-permute-start.2 = (bf16[8,6,128]{2,0,1:T(8,128)(2,1)S(1)}, bf16[8,6,128]{2,0,1:T(8,128)(2,1)S(1)}, u32[]{:S(2)}, u32[]{:S(2)}) collective-permute-start(bf16[8,6,128]{2,0,1:T(8,128)(2,1)S(1)} %slice.91), channel_id=1, source_target_pairs={{24,0},{32,8},{40,16},{48,24},{56,32},{64,40},{72,48},{80,56},{88,... | collective-permute-start | bytes 36872 | tf_op jit(solution)/shard_map/ppermute | solution.py:14
  3.6 27.9 %collective-permute-start.1 = (bf16[8,6,128]{2,0,1:T(8,128)(2,1)S(1)}, bf16[8,6,128]{2,0,1:T(8,128)(2,1)S(1)}, u32[]{:S(2)}, u32[]{:S(2)}) collective-permute-start(bf16[8,6,128]{2,0,1:T(8,128)(2,1)S(1)} %slice.91), channel_id=1, source_target_pairs={{16,0},{24,8},{32,16},{40,24},{48,32},{56,40},{64,48},{72,56},{80,... | collective-permute-start | bytes 36872 | tf_op jit(solution)/shard_map/ppermute | solution.py:14
  4.9 26.6 %collective-permute-start = (bf16[8,6,128]{2,0,1:T(8,128)(2,1)S(1)}, bf16[8,6,128]{2,0,1:T(8,128)(2,1)S(1)}, u32[]{:S(2)}, u32[]{:S(2)}) collective-permute-start(bf16[8,6,128]{2,0,1:T(8,128)(2,1)S(1)} %slice.91), channel_id=1, source_target_pairs={{8,0},{16,8},{24,16},{32,24},{40,32},{48,40},{56,48},{64,56},{72,6... | collective-permute-start | bytes 36872 | tf_op jit(solution)/shard_map/ppermute | solution.py:14
  14.3 17.4 %copy-start.1 = (bf16[128,128,128]{2,1,0:T(8,128)(2,1)S(1)}, bf16[128,128,128]{2,1,0:T(8,128)(2,1)}, u32[]{:S(2)}) copy-start(bf16[128,128,128]{2,1,0:T(8,128)(2,1)} %param.16) | copy-start | bytes 12582916
  20.1 35.9 %copy-start.2 = (f32[8,2048]{1,0:T(8,128)S(1)}, f32[8,2048]{1,0:T(8,128)}, u32[]{:S(2)}) copy-start(f32[8,2048]{1,0:T(8,128)} %param.13) | copy-start | bytes 196612
  20.2 14.7 %collective-permute-start.5 = (f32[8,6,128]{2,0,1:T(8,128)S(1)}, f32[8,6,128]{2,0,1:T(8,128)S(1)}, u32[]{:S(2)}, u32[]{:S(2)}) collective-permute-start(f32[8,6,128]{2,0,1:T(8,128)S(1)} %get-tuple-element.40), channel_id=1, source_target_pairs={{0,24},{8,32},{16,40},{24,48},{32,56},{40,64},{48,72},{56,80},{64,... | collective-permute-start | bytes 73736 | tf_op jit(solution)/shard_map/ppermute | solution.py:14
  26.2 8.7 %collective-permute-start.4 = (f32[8,6,128]{2,0,1:T(8,128)S(1)}, f32[8,6,128]{2,0,1:T(8,128)S(1)}, u32[]{:S(2)}, u32[]{:S(2)}) collective-permute-start(f32[8,6,128]{2,0,1:T(8,128)S(1)} %get-tuple-element.41), channel_id=1, source_target_pairs={{0,16},{8,24},{16,32},{24,40},{32,48},{40,56},{48,64},{56,72},{64,... | collective-permute-start | bytes 73736 | tf_op jit(solution)/shard_map/ppermute | solution.py:14
  29.5 5.3 %collective-permute-start.3 = (f32[8,6,128]{2,0,1:T(8,128)S(1)}, f32[8,6,128]{2,0,1:T(8,128)S(1)}, u32[]{:S(2)}, u32[]{:S(2)}) collective-permute-start(f32[8,6,128]{2,0,1:T(8,128)S(1)} %get-tuple-element.42), channel_id=1, source_target_pairs={{0,8},{8,16},{16,24},{24,32},{32,40},{40,48},{48,56},{56,64},{64,7... | collective-permute-start | bytes 73736 | tf_op jit(solution)/shard_map/ppermute | solution.py:14
